TPU v7x, 256 devices: a whole 4x4x8 slice. The times are simulated.
256 devices in a mesh: seq: 64 (over x, z, core), tp: 4 (over y).
Axes of the slice: x: 4, y: 4, z: 8, core: 2. Of those that a mesh axis runs over, the one named last changes fastest.
Arguments:
- token_ids: int32 [65536], P('seq'), may hold values from 0 to 511
- embed_table: bfloat16 [512, 2048], P(None, 'tp'), may hold values from -6 to 6
- norm_gain: float32 [2048], replicated, may hold values from 0.1 to 1.9
- in_weight: bfloat16 [2048, 3, 2048], P('seq', None, 'tp'), may hold values from -0.125 to 0.125
- short_filter: float32 [7, 3, 2048], P(None, None, 'tp'), may hold values from -2.4 to 2.4
- long_filter: bfloat16 [128, 128], P('tp'), may hold values from -0.5390625 to 0.5390625
- long_skip: float32 [2048], P('tp'), may hold values from -3 to 3
- out_weight: bfloat16 [2048, 2048], P('tp', 'seq'), may hold values from -0.125 to 0.125
Outputs:
- mixed: bfloat16 [65536, 2048], P('seq', 'tp')
All inputs are finite; a program needn't handle non-finite values.
Results may differ from a plain program's by a relative error of at most 0.012.
Values may be sent and summed in bfloat16 or wider, within the bound.
A program may use at most 64 MiB of HBM per device.

v0:
```python
import jax
import jax.numpy as jnp
from jax import lax
from jax.sharding import PartitionSpec as P


def from_behind(block, axis, distance):
    devices = range(lax.axis_size(axis))
    route = [(i - distance, i) for i in devices if i - distance in devices]
    return lax.ppermute(block, axis, route)


def short_conv(extended, short_filter, out_length):
    short_taps = short_filter.shape[0]
    running = jnp.zeros((out_length,) + extended.shape[1:], jnp.float32)
    for tap_index in range(short_taps):
        begin = short_taps - 1 - tap_index
        running = running + short_filter[tap_index][None] * extended[
            begin : begin + out_length
        ].astype(jnp.float32)
    return running


def body(
    token_ids, embed_table, norm_gain, in_weight, short_filter, long_filter, long_skip, out_weight
):
    tok_count = token_ids.shape[0]
    vocab_size = embed_table.shape[0]
    local_width = embed_table.shape[1]
    onehot = (token_ids[:, None] == jnp.arange(vocab_size, dtype=jnp.int32)[None, :]).astype(
        jnp.bfloat16
    )
    own_feats = jnp.dot(onehot, embed_table, preferred_element_type=jnp.float32).astype(
        jnp.bfloat16
    )
    features = lax.all_gather(own_feats, "tp", axis=1, tiled=True)
    widened = features.astype(jnp.float32)
    scaled = (
        widened
        * lax.rsqrt(jnp.mean(widened * widened, axis=1, keepdims=True) + 1e-06)
        * norm_gain[None, :]
    )
    normed = scaled.astype(jnp.bfloat16)
    projected = jnp.einsum(
        "td,dsc->tsc",
        normed,
        lax.all_gather(in_weight, "seq", axis=0, tiled=True),
        preferred_element_type=jnp.float32,
    ).astype(jnp.bfloat16)
    tap_count = long_filter.shape[1]
    short_taps = short_filter.shape[0]
    rim_rows = from_behind(projected[tok_count - short_taps + 1 :], "seq", 1)
    extended = jnp.concatenate([rim_rows, projected], axis=0)
    featured = short_conv(extended, short_filter, tok_count)
    queries = featured[:, 0]
    gated_kv = (featured[:, 1] * featured[:, 2]).astype(jnp.bfloat16)
    earlier = from_behind(gated_kv[tok_count - tap_count :], "seq", 1)
    product = jnp.concatenate([earlier, gated_kv], axis=0)
    groups_here = long_filter.shape[0]
    group_size = local_width // groups_here
    positions = jnp.arange(tap_count, dtype=jnp.int32)
    differ = positions[:, None, None] - positions[None, :, None]
    target = positions[None, None, :]
    near_pick = (differ == target).astype(jnp.float32)
    far_pick = (differ + tap_count == target).astype(jnp.float32)
    filter_f32 = long_filter.astype(jnp.float32)
    near_band = jnp.einsum("isj,gj->gis", near_pick, filter_f32).astype(jnp.bfloat16)
    far_band = jnp.einsum("isj,gj->gis", far_pick, filter_f32).astype(jnp.bfloat16)
    blocks = product.reshape(tok_count // tap_count + 1, tap_count, groups_here, group_size)
    convolved = jnp.einsum(
        "gis,bsgc->bigc", near_band, blocks[1:], preferred_element_type=jnp.float32
    )
    convolved = convolved + jnp.einsum(
        "gis,bsgc->bigc", far_band, blocks[:-1], preferred_element_type=jnp.float32
    )
    convolved = convolved.reshape(tok_count, local_width) + long_skip[None, :] * product[
        tap_count:
    ].astype(jnp.float32)
    gated = (queries * convolved).astype(jnp.bfloat16)
    partials = jnp.dot(
        gated,
        lax.all_gather(out_weight, "seq", axis=1, tiled=True),
        preferred_element_type=jnp.float32,
    )
    summed = lax.psum(partials.astype(jnp.bfloat16), "tp").astype(jnp.float32)
    own_share = lax.dynamic_slice_in_dim(summed, lax.axis_index("tp") * local_width, local_width, 1)
    return (own_feats.astype(jnp.float32) + own_share).astype(jnp.bfloat16)


def solution(mesh):
    placed = (
        P("seq"),
        P(None, "tp"),
        P(),
        P("seq", None, "tp"),
        P(None, None, "tp"),
        P("tp", None),
        P("tp"),
        P("tp", "seq"),
    )
    return jax.shard_map(
        body, mesh=mesh, in_specs=placed, out_specs=P("seq", "tp"), check_vma=False
    )
```

profile of v0, /device:TPU:1, one launch (start us, length us, event | category | flops | bytes accessed | tf_op | source)
XLA Modules:
  0.0 337.5 jit_solution(16231888260444834584)
XLA Ops:
  6.5 0.0 copy-start
  6.5 0.0 all-gather.4.cloned.1.call-start
  6.5 1.0 copy-done
  7.6 2.4 fusion.24
  10.0 0.0 all-gather.4.cloned.1.call-update
  10.0 0.0 all-gather.6.cloned.1.call-start
  10.1 0.7 all-gather.6.cloned.1.call-update
  10.8 0.0 all-gather.8.cloned.1.call-start
  10.8 0.7 all-gather.8.cloned.1.call-update
  11.5 0.0 all-reduce.2.cloned.1.call-start
  11.6 1.2 fusion.38
  12.8 0.0 copy-start.6
  12.8 5.8 %fusion.3 = bf16[128,128,32]{1,2,0:T(8,128)(2,1)} fusion(s32[128,128]{1,0:T(8,128)S(1)} %iota_subtract_fusion, bf16[32,128]{1,0:T(8,128)(2,1)} %param.13), kind=kOutput, calls=%fused_computation.7 | convolution fusion | flops 136314880 | bytes 1122304 | tf_op jit(solution)/shard_map/isj,gj->gis/dot_general | solution.py:67
  18.6 0.0 copy-done.5
  18.6 5.1 %fusion.4 = bf16[128,128,32]{1,2,0:T(8,128)(2,1)} fusion(s32[128,128]{1,0:T(8,128)S(1)} %broadcast_add_fusion, bf16[32,128]{1,0:T(8,128)(2,1)S(1)} %copy-done.5), kind=kOutput, calls=%fused_computation.8 | convolution fusion | flops 136314880 | bytes 1122304 | tf_op jit(solution)/shard_map/isj,gj->gis/dot_general | solution.py:68
  23.7 40.8 %all-gather.4.cloned.1.call-done = bf16[1024,2048]{1,0:T(8,128)(2,1)} async-done(((bf16[1024,512]{1,0:T(8,128)(2,1)}), bf16[1024,2048]{1,0:T(8,128)(2,1)}) %all-gather.4.cloned.1.call-update) | async-done | bytes 4194320 | tf_op jit(solution)/shard_map/all_gather | solution.py:36
  64.6 3.1 fusion
  67.7 81.2 %all-gather.6.cloned.1.call-done = bf16[2048,3,512]{2,0,1:T(8,128)(2,1)} async-done(((bf16[32,3,512]{2,0,1:T(8,128)(2,1)}), bf16[2048,3,512]{2,0,1:T(8,128)(2,1)}) %all-gather.6.cloned.1.call-update) | async-done | bytes 6291472 | tf_op jit(solution)/shard_map/all_gather | solution.py:47
  148.8 0.0 copy-done.6
  148.8 10.5 %fusion.17 = bf16[1024,3,512]{2,0,1:T(8,128)(2,1)S(1)} fusion(bf16[2048,3,512]{2,0,1:T(8,128)(2,1)} %all-gather.6.cloned.1.call-done, bf16[1024,2048]{1,0:T(8,128)(2,1)} %all-gather.4.cloned.1.call-done, f32[2048]{0:T(1024)S(1)} %copy-done.6, f32[1024]{0:T(1024)S(1)} %add_rsqrt_fusion), kind=kOutput, calls=%fused_computation.31 | convolution fusion | flops 6452412416 | bytes 13643776 | tf_op jit(solution)/shard_map/td,dsc->tsc/dot_general | solution.py:44
  159.4 2.8 collective-permute-start
  162.2 0.9 collective-permute-done
  163.1 5.6 %multiply_add_fusion = f32[1024,3,512]{2,0,1:T(8,128)S(1)} fusion(bf16[1024,3,512]{2,0,1:T(8,128)(2,1)S(1)} %fusion.17, bf16[6,3,512]{2,0,1:T(8,128)(2,1)S(1)} %collective-permute-done, f32[3,512]{1,0:T(4,128)S(1)} %get-tuple-element.12, f32[3,512]{1,0:T(4,128)S(1)} %get-tuple-element.13, f32[3,512]{1,0:T(4,128)S(1)} %get-tuple-element.14, ...), kind=kLoop, calls=%fused_computation.14 | loop fusion | flops 59768832 | bytes 9498624 | tf_op jit(solution)/shard_map/add | solution.py:18
  168.7 0.0 copy-start.1
  168.7 2.7 copy-done.1
  171.3 0.4 fusion.20
  171.7 0.0 copy-start.3
  171.7 0.5 copy.12
  172.2 0.0 copy-start.2
  172.3 4.7 %collective-permute-start.1 = (bf16[128,512]{1,0:T(8,128)(2,1)S(1)}, bf16[128,512]{1,0:T(8,128)(2,1)S(1)}, u32[]{:S(2)}, u32[]{:S(2)}) collective-permute-start(bf16[128,512]{1,0:T(8,128)(2,1)S(1)} %slice_bitcast_fusion.1), channel_id=1, source_target_pairs={{0,4},{4,8},{8,12},{12,16},{16,20},{20,24},{24,28},{28,32},{32,36}... | collective-permute-start | bytes 393224 | tf_op jit(solution)/shard_map/ppermute | solution.py:10
  176.9 0.3 copy.29
  177.2 0.0 copy-done.3
  177.2 2.1 fusion.26
  179.3 0.4 fusion.42
  179.7 0.0 collective-permute-done.1
  179.7 1.1 pad_maximum_fusion.1
  180.7 2.3 copy.14
  183.0 1.5 copy.30
  184.5 2.1 add_bitcast_fusion
  186.6 0.0 copy-start.7
  186.6 0.9 copy.16
  187.5 0.5 copy.52
  188.0 1.8 copy.17
  189.8 35.9 %all-gather.8.cloned.1.call-done = bf16[512,2048]{0,1:T(8,128)(2,1)} async-done(((bf16[512,32]{0,1:T(8,128)(2,1)}), bf16[512,2048]{0,1:T(8,128)(2,1)}) %all-gather.8.cloned.1.call-update) | async-done | bytes 2097168 | tf_op jit(solution)/shard_map/all_gather | solution.py:82
  225.7 7.6 %convolution_convert_fusion = bf16[1024,2048]{1,0:T(8,128)(2,1)} fusion(bf16[512,2048]{0,1:T(8,128)(2,1)} %all-gather.8.cloned.1.call-done, f32[1024,3,512]{2,0,1:T(8,128)} %copy-done.1, f32[1024,512]{1,0:T(8,128)} %copy.17, f32[512]{0:T(512)S(1)} %copy-done.7, bf16[1024,1,512]{2,0,1:T(8,128)(2,1)} %copy-done.3), kind=kOutput, calls=%fused_computation.21 | convolution fusion | flops 2152202240 | bytes 11536384 | tf_op jit(solution)/shard_map/dot_general | solution.py:80
  233.3 0.0 all-reduce.2.cloned.1.call-update
  233.3 95.2 %all-reduce.2.cloned.1.call-done = bf16[1024,2048]{1,0:T(8,128)(2,1)} async-done(((bf16[1024,2048]{1,0:T(8,128)(2,1)}), bf16[1024,2048]{1,0:T(8,128)(2,1)}) %all-reduce.2.cloned.1.call-update) | async-done | bytes 4194320 | tf_op jit(solution)/shard_map/psum | solution.py:85
  328.5 2.5 add_convert_fusion
  (14 shorter events, 0.1 us)
Async XLA Ops:
  6.5 1.0 copy-start
  6.5 12.1 %copy-start.5 = (bf16[32,128]{1,0:T(8,128)(2,1)S(1)}, bf16[32,128]{1,0:T(8,128)(2,1)}, u32[]{:S(2)}) copy-start(bf16[32,128]{1,0:T(8,128)(2,1)} %param.13) | copy-start | bytes 24580
  6.5 58.0 %all-gather.4.cloned.1.call-start = ((), (), s32[]{:S(2)}) async-start(), calls=%async_computation | async-start | bytes 5242880 | tf_op jit(solution)/shard_map/all_gather | solution.py:36
  10.0 138.8 %all-gather.6.cloned.1.call-start = ((), (), s32[]{:S(2)}) async-start(), calls=%async_computation.1 | async-start | bytes 6389760 | tf_op jit(solution)/shard_map/all_gather | solution.py:47
  10.8 214.9 %all-gather.8.cloned.1.call-start = ((), (), s32[]{:S(2)}) async-start(), calls=%async_computation.2 | async-start | bytes 2129920 | tf_op jit(solution)/shard_map/all_gather | solution.py:82
  11.5 317.0 %all-reduce.2.cloned.1.call-start = ((), (), s32[]{:S(2)}) async-start(), calls=%async_computation.3 | async-start | bytes 8388608 | tf_op jit(solution)/shard_map/psum | solution.py:85
  12.8 136.0 %copy-start.6 = (f32[2048]{0:T(1024)S(1)}, f32[2048]{0:T(1024)}, u32[]{:S(2)}) copy-start(f32[2048]{0:T(1024)} %param.10) | copy-start | bytes 24580
  159.4 3.7 %collective-permute-start = (bf16[6,3,512]{2,0,1:T(8,128)(2,1)S(1)}, bf16[6,3,512]{2,0,1:T(8,128)(2,1)S(1)}, u32[]{:S(2)}, u32[]{:S(2)}) collective-permute-start(bf16[6,3,512]{2,0,1:T(8,128)(2,1)S(1)} %slice.86), channel_id=1, source_target_pairs={{0,4},{4,8},{8,12},{12,16},{16,20},{20,24},{24,28},{28,32},{32,36}... | collective-permute-start | bytes 55304 | tf_op jit(solution)/shard_map/ppermute | solution.py:10
  168.7 2.7 copy-start.1
  171.7 5.5 %copy-start.3 = (bf16[1024,1,512]{2,0,1:T(8,128)(2,1)}, bf16[1024,1,512]{2,0,1:T(8,128)(2,1)S(1)}, u32[]{:S(2)}) copy-start(bf16[1024,1,512]{2,0,1:T(8,128)(2,1)S(1)} %fusion.20) | copy-start | bytes 3145732
  172.2 7.1 %copy-start.2 = (f32[1024,3,512]{2,0,1:T(8,128)S(1)}, f32[1024,3,512]{2,0,1:T(8,128)}, u32[]{:S(2)}) copy-start(f32[1024,3,512]{2,0,1:T(8,128)} %copy-done.1) | copy-start | bytes 18874372
  172.3 7.4 %collective-permute-start.1 = (bf16[128,512]{1,0:T(8,128)(2,1)S(1)}, bf16[128,512]{1,0:T(8,128)(2,1)S(1)}, u32[]{:S(2)}, u32[]{:S(2)}) collective-permute-start(bf16[128,512]{1,0:T(8,128)(2,1)S(1)} %slice_bitcast_fusion.1), channel_id=1, source_target_pairs={{0,4},{4,8},{8,12},{12,16},{16,20},{20,24},{24,28},{28,32},{32,36}... | collective-permute-start | bytes 393224 | tf_op jit(solution)/shard_map/ppermute | solution.py:10
  186.6 39.1 %copy-start.7 = (f32[512]{0:T(512)S(1)}, f32[512]{0:T(512)}, u32[]{:S(2)}) copy-start(f32[512]{0:T(512)} %param.14) | copy-start | bytes 6148
  189.8 138.7 %copy-start.4 = (bf16[1024,512]{1,0:T(8,128)(2,1)S(1)}, bf16[1024,512]{1,0:T(8,128)(2,1)}, u32[]{:S(2)}) copy-start(bf16[1024,512]{1,0:T(8,128)(2,1)} %fusion.24) | copy-start | bytes 3145732
Sparse Core Ops, SparseCore 0:
  10.1 54.3 all-gather.3
  67.4 81.3 all-gather.5
  151.6 74.0 all-gather.7
  233.4 94.9 all-reduce.1
where the time goes:
time: 338 us; the launch traced here: 337 us
  waiting for transfers between devices  255 us (75%)
  matrix products  35.6 us (11%)
  between operations  13.3 us (4%)
  other arithmetic  12.9 us (4%)
  local copies, waits for them, and re-layouts  12.7 us (4%)
  starting transfers between devices  7.53 us (2%)
    psum x1, waiting for transfers between devices, body(): summed = lax.psum(partials.astype(jnp.bfloat16), 'tp').astype(jnp.float32)  95.2 us
    all_gather x1, waiting for transfers between devices, body(): lax.all_gather(in_weight, 'seq', axis=0, tiled=True)  81.2 us
    all_gather x1, waiting for transfers between devices, body(): features = lax.all_gather(own_feats, 'tp', axis=1, tiled=True)  40.8 us
    all_gather x1, waiting for transfers between devices, body(): lax.all_gather(out_weight, 'seq', axis=1, tiled=True)  35.9 us
    dot_general x1, matrix products, body(): jnp.einsum('td,dsc->tsc', normed, lax.all_gather(in_weight, 'seq', axis=0...  10.5 us
    dot_general x1, matrix products, body(): jnp.dot(gated, lax.all_gather(out_weight, 'seq', axis=1, tiled=True), pre...  7.59 us
    ppermute x2, starting transfers between devices, from_behind(): return lax.ppermute(block, axis, route)  7.41 us
  transfers between devices with their start and end apart: 6, of which 5 were waited for; matrix products, arithmetic and copies ran while one was open for 13% of the time, Pallas kernels for 0%

commit v1 on v0

--- a/solution.py
+++ b/solution.py
@@ -82,7 +82,9 @@
         lax.all_gather(out_weight, "seq", axis=1, tiled=True),
         preferred_element_type=jnp.float32,
     )
-    summed = lax.psum(partials.astype(jnp.bfloat16), "tp").astype(jnp.float32)
+    summed = jnp.sum(lax.all_gather(partials.astype(jnp.bfloat16), "tp"), axis=0).astype(
+        jnp.float32
+    )
     own_share = lax.dynamic_slice_in_dim(summed, lax.axis_index("tp") * local_width, local_width, 1)
     return (own_feats.astype(jnp.float32) + own_share).astype(jnp.bfloat16)
 

time: 338 us -> 409 us (1.21)
  waiting for transfers between devices: 255 us -> 314 us
  other arithmetic: 12.9 us -> 25 us
    all_gather x0 -> x1, waiting for transfers between devices: none -> 154 us  [body(): lax.all_gather(partials.astype(jnp.bfloat16), 'tp')]
    psum x1 -> x0, waiting for transfers between devices: 95.2 us -> none  [body(): summed = lax.psum(partials.astype(jnp.bfloat16), 'tp').astype(jnp.float32)]
    reduce_sum x0 -> x1, other arithmetic: none -> 12 us  [body(): jnp.sum(lax.all_gather(partials.astype(jnp.bfloat16), 'tp'), axis=0)]
  transfers between devices with their start and end apart: 6 -> 6, of which waited for: 5 -> 5; matrix products, arithmetic and copies ran while one was open for 13% -> 11% of each run, Pallas kernels for 0% -> 0%
where the time goes in v1:
time: 409 us; the launch traced here: 408 us
  waiting for transfers between devices  314 us (77%)
  matrix products  35.5 us (9%)
  other arithmetic  25 us (6%)
  between operations  13.3 us (3%)
  local copies, waits for them, and re-layouts  12.8 us (3%)
  starting transfers between devices  7.51 us (2%)
    all_gather x1, waiting for transfers between devices, body(): lax.all_gather(partials.astype(jnp.bfloat16), 'tp')  154 us
    all_gather x1, waiting for transfers between devices, body(): lax.all_gather(in_weight, 'seq', axis=0, tiled=True)  81.2 us
    all_gather x1, waiting for transfers between devices, body(): features = lax.all_gather(own_feats, 'tp', axis=1, tiled=True)  40.9 us
    all_gather x1, waiting for transfers between devices, body(): lax.all_gather(out_weight, 'seq', axis=1, tiled=True)  35.8 us
    reduce_sum x1, other arithmetic, body(): jnp.sum(lax.all_gather(partials.astype(jnp.bfloat16), 'tp'), axis=0)  12 us
    dot_general x1, matrix products, body(): jnp.einsum('td,dsc->tsc', normed, lax.all_gather(in_weight, 'seq', axis=0...  10.5 us
  transfers between devices with their start and end apart: 6, of which 5 were waited for; matrix products, arithmetic and copies ran while one was open for 11% of the time, Pallas kernels for 0%

profile of v1, /device:TPU:1, one launch (start us, length us, event | category | flops | bytes accessed | tf_op | source)
XLA Modules:
  0.0 408.2 jit_solution(3148416070523768225)
XLA Ops:
  6.5 0.0 copy-start
  6.5 0.0 all-gather.6.cloned.1.call-start
  6.5 1.0 copy-done
  7.6 2.4 fusion.24
  10.0 0.0 all-gather.6.cloned.1.call-update
  10.0 0.0 all-gather.8.cloned.1.call-start
  10.1 0.7 all-gather.8.cloned.1.call-update
  10.8 0.0 all-gather.10.cloned.1.call-start
  10.8 0.7 all-gather.10.cloned.1.call-update
  11.5 0.0 all-gather.12.cloned.1.call-start
  11.6 1.2 fusion.38
  12.8 0.0 copy-start.7
  12.8 5.8 %fusion.3 = bf16[128,128,32]{1,2,0:T(8,128)(2,1)} fusion(s32[128,128]{1,0:T(8,128)S(1)} %iota_subtract_fusion, bf16[32,128]{1,0:T(8,128)(2,1)} %param.13), kind=kOutput, calls=%fused_computation.7 | convolution fusion | flops 136314880 | bytes 1122304 | tf_op jit(solution)/shard_map/isj,gj->gis/dot_general | solution.py:67
  18.6 0.0 copy-done.6
  18.6 5.1 %fusion.4 = bf16[128,128,32]{1,2,0:T(8,128)(2,1)} fusion(s32[128,128]{1,0:T(8,128)S(1)} %broadcast_add_fusion, bf16[32,128]{1,0:T(8,128)(2,1)S(1)} %copy-done.6), kind=kOutput, calls=%fused_computation.8 | convolution fusion | flops 136314880 | bytes 1122304 | tf_op jit(solution)/shard_map/isj,gj->gis/dot_general | solution.py:68
  23.7 40.9 %all-gather.6.cloned.1.call-done = bf16[1024,2048]{1,0:T(8,128)(2,1)} async-done(((bf16[1024,512]{1,0:T(8,128)(2,1)}), bf16[1024,2048]{1,0:T(8,128)(2,1)}) %all-gather.6.cloned.1.call-update) | async-done | bytes 4194320 | tf_op jit(solution)/shard_map/all_gather | solution.py:36
  64.6 3.1 fusion
  67.7 81.2 %all-gather.8.cloned.1.call-done = bf16[2048,3,512]{2,0,1:T(8,128)(2,1)} async-done(((bf16[32,3,512]{2,0,1:T(8,128)(2,1)}), bf16[2048,3,512]{2,0,1:T(8,128)(2,1)}) %all-gather.8.cloned.1.call-update) | async-done | bytes 6291472 | tf_op jit(solution)/shard_map/all_gather | solution.py:47
  148.9 0.0 copy-done.7
  148.9 10.5 %fusion.17 = bf16[1024,3,512]{2,0,1:T(8,128)(2,1)S(1)} fusion(bf16[2048,3,512]{2,0,1:T(8,128)(2,1)} %all-gather.8.cloned.1.call-done, bf16[1024,2048]{1,0:T(8,128)(2,1)} %all-gather.6.cloned.1.call-done, f32[2048]{0:T(1024)S(1)} %copy-done.7, f32[1024]{0:T(1024)S(1)} %add_rsqrt_fusion), kind=kOutput, calls=%fused_computation.31 | convolution fusion | flops 6452412416 | bytes 13643776 | tf_op jit(solution)/shard_map/td,dsc->tsc/dot_general | solution.py:44
  159.5 2.7 collective-permute-start
  162.2 0.9 collective-permute-done
  163.1 5.6 %multiply_add_fusion = f32[1024,3,512]{2,0,1:T(8,128)S(1)} fusion(bf16[1024,3,512]{2,0,1:T(8,128)(2,1)S(1)} %fusion.17, bf16[6,3,512]{2,0,1:T(8,128)(2,1)S(1)} %collective-permute-done, f32[3,512]{1,0:T(4,128)S(1)} %get-tuple-element.12, f32[3,512]{1,0:T(4,128)S(1)} %get-tuple-element.13, f32[3,512]{1,0:T(4,128)S(1)} %get-tuple-element.14, ...), kind=kLoop, calls=%fused_computation.14 | loop fusion | flops 59768832 | bytes 9498624 | tf_op jit(solution)/shard_map/add | solution.py:18
  168.7 0.0 copy-start.2
  168.8 2.7 copy-done.2
  171.4 0.4 fusion.20
  171.8 0.0 copy-start.4
  171.8 0.5 copy.12
  172.3 4.7 %collective-permute-start.1 = (bf16[128,512]{1,0:T(8,128)(2,1)S(1)}, bf16[128,512]{1,0:T(8,128)(2,1)S(1)}, u32[]{:S(2)}, u32[]{:S(2)}) collective-permute-start(bf16[128,512]{1,0:T(8,128)(2,1)S(1)} %slice_bitcast_fusion.1), channel_id=1, source_target_pairs={{0,4},{4,8},{8,12},{12,16},{16,20},{20,24},{24,28},{28,32},{32,36}... | collective-permute-start | bytes 393224 | tf_op jit(solution)/shard_map/ppermute | solution.py:10
  177.0 0.3 copy.29
  177.3 2.1 fusion.26
  179.4 0.4 fusion.42
  179.7 0.0 collective-permute-done.1
  179.8 1.1 pad_maximum_fusion.1
  180.8 2.3 copy.14
  183.1 1.5 copy.30
  184.6 2.1 add_bitcast_fusion
  186.7 0.0 copy-start.8
  186.7 0.9 copy.16
  187.6 0.5 copy.52
  188.0 1.9 copy.17
  189.9 35.8 %all-gather.10.cloned.1.call-done = bf16[512,2048]{0,1:T(8,128)(2,1)} async-done(((bf16[512,32]{0,1:T(8,128)(2,1)}), bf16[512,2048]{0,1:T(8,128)(2,1)}) %all-gather.10.cloned.1.call-update) | async-done | bytes 2097168 | tf_op jit(solution)/shard_map/all_gather | solution.py:82
  225.8 7.5 %convolution_convert_fusion = bf16[1024,2048]{1,0:T(8,128)(2,1)} fusion(bf16[512,2048]{0,1:T(8,128)(2,1)} %all-gather.10.cloned.1.call-done, f32[1024,3,512]{2,0,1:T(8,128)} %copy-done.2, f32[1024,512]{1,0:T(8,128)} %copy.17, f32[512]{0:T(512)S(1)} %copy-done.8, bf16[1024,1,512]{2,0,1:T(8,128)(2,1)} %copy-done.4), kind=kOutput, calls=%fused_computation.21 | convolution fusion | flops 2152202240 | bytes 11536384 | tf_op jit(solution)/shard_map/dot_general | solution.py:80
  233.3 0.0 all-gather.12.cloned.1.call-update
  233.3 153.8 %all-gather.12.cloned.1.call-done = bf16[4096,2048]{1,0:T(8,128)(2,1)} async-done(((bf16[1024,2048]{1,0:T(8,128)(2,1)}), bf16[4096,2048]{1,0:T(8,128)(2,1)}) %all-gather.12.cloned.1.call-update) | async-done | bytes 16777232 | tf_op jit(solution)/shard_map/all_gather | solution.py:85
  387.1 12.0 %reduce_sum.22 = bf16[1024,2048]{1,0:T(8,128)(2,1)} reduce(bf16[4,1024,2048]{2,1,0:T(8,128)(2,1)} %bitcast.78, bf16[]{:T(256)} %constant.7.clone.1), dimensions={0}, to_apply=%region_1.0 | reduce | flops 6291456 | bytes 20971522 | tf_op jit(solution)/shard_map/reduce_sum | solution.py:85
  399.1 0.0 copy-done.5
  399.1 2.5 add_convert_fusion
  (17 shorter events, 0.1 us)
Async XLA Ops:
  6.5 1.0 copy-start
  6.5 12.0 %copy-start.6 = (bf16[32,128]{1,0:T(8,128)(2,1)S(1)}, bf16[32,128]{1,0:T(8,128)(2,1)}, u32[]{:S(2)}) copy-start(bf16[32,128]{1,0:T(8,128)(2,1)} %param.13) | copy-start | bytes 24580
  6.5 58.1 %all-gather.6.cloned.1.call-start = ((), (), s32[]{:S(2)}) async-start(), calls=%async_computation | async-start | bytes 5242880 | tf_op jit(solution)/shard_map/all_gather | solution.py:36
  10.0 138.9 %all-gather.8.cloned.1.call-start = ((), (), s32[]{:S(2)}) async-start(), calls=%async_computation.1 | async-start | bytes 6389760 | tf_op jit(solution)/shard_map/all_gather | solution.py:47
  10.8 215.0 %all-gather.10.cloned.1.call-start = ((), (), s32[]{:S(2)}) async-start(), calls=%async_computation.2 | async-start | bytes 2129920 | tf_op jit(solution)/shard_map/all_gather | solution.py:82
  11.5 375.6 %all-gather.12.cloned.1.call-start = ((), (), s32[]{:S(2)}) async-start(), calls=%async_computation.3 | async-start | bytes 20971520 | tf_op jit(solution)/shard_map/all_gather | solution.py:85
  12.8 136.1 %copy-start.7 = (f32[2048]{0:T(1024)S(1)}, f32[2048]{0:T(1024)}, u32[]{:S(2)}) copy-start(f32[2048]{0:T(1024)} %param.10) | copy-start | bytes 24580
  159.5 3.7 collective-permute-start
  168.7 2.7 copy-start.2
  171.8 5.5 %copy-start.4 = (bf16[1024,1,512]{2,0,1:T(8,128)(2,1)}, bf16[1024,1,512]{2,0,1:T(8,128)(2,1)S(1)}, u32[]{:S(2)}) copy-start(bf16[1024,1,512]{2,0,1:T(8,128)(2,1)S(1)} %fusion.20) | copy-start | bytes 3145732
  172.3 7.1 %copy-start.3 = (f32[1024,3,512]{2,0,1:T(8,128)S(1)}, f32[1024,3,512]{2,0,1:T(8,128)}, u32[]{:S(2)}) copy-start(f32[1024,3,512]{2,0,1:T(8,128)} %copy-done.2) | copy-start | bytes 18874372
  172.3 7.4 %collective-permute-start.1 = (bf16[128,512]{1,0:T(8,128)(2,1)S(1)}, bf16[128,512]{1,0:T(8,128)(2,1)S(1)}, u32[]{:S(2)}, u32[]{:S(2)}) collective-permute-start(bf16[128,512]{1,0:T(8,128)(2,1)S(1)} %slice_bitcast_fusion.1), channel_id=1, source_target_pairs={{0,4},{4,8},{8,12},{12,16},{16,20},{20,24},{24,28},{28,32},{32,36}... | collective-permute-start | bytes 393224 | tf_op jit(solution)/shard_map/ppermute | solution.py:10
  186.7 39.1 %copy-start.8 = (f32[512]{0:T(512)S(1)}, f32[512]{0:T(512)}, u32[]{:S(2)}) copy-start(f32[512]{0:T(512)} %param.14) | copy-start | bytes 6148
  387.1 12.0 %copy-start.5 = (bf16[1024,512]{1,0:T(8,128)(2,1)S(1)}, bf16[1024,512]{1,0:T(8,128)(2,1)}, u32[]{:S(2)}) copy-start(bf16[1024,512]{1,0:T(8,128)(2,1)} %fusion.24) | copy-start | bytes 3145732
  387.1 14.5 %copy-start.1 = (bf16[512,512]{1,0:T(8,128)(2,1)S(1)}, bf16[512,512]{1,0:T(8,128)(2,1)}, u32[]{:S(2)}) copy-start(bf16[512,512]{1,0:T(8,128)(2,1)} %param.9) | copy-start | bytes 1572868
Sparse Core Ops, SparseCore 0:
  10.1 54.4 all-gather.5
  67.4 81.4 all-gather.7
  151.7 74.0 all-gather.9
  233.4 153.6 all-gather.11
